TPU v7x, 32 devices: a whole 2x2x4 slice. The times are simulated.
32 devices in a mesh: region: 4 (over y, x), cluster: 8 (over z, core).
Axes of the slice: x: 2, y: 2, z: 4, core: 2. Of those that a mesh axis runs over, the one named last changes fastest.
Arguments:
- pilots: bfloat16 [128, 1024, 1024], P(('region', 'cluster')), may hold values from -0.1875 to 0.1875
- estimate: bfloat16 [128, 8, 1024], P(('region', 'cluster')), may hold values from -6 to 6
- visible: int32 [128, 1024], P(('region', 'cluster')), may hold values from 0 to 65535, as said below
- blocks: int32 [128], P(('region', 'cluster')), may hold values from 4 to 8
- received: float32 [128, 8, 1024], P(('region', 'cluster')), may hold values from -6 to 6
- previous: float32 [128, 8, 1024], P(('region', 'cluster')), may hold values from -6 to 6
- onsager: float32 [128], P(('region', 'cluster')), may hold values from 0.2 to 0.8
- user_cluster: int32 [65536], replicated, may hold values from 0 to 15
- cluster_prior: float32 [16], replicated, may hold values from -4 to 0
Outputs:
- new_estimate: bfloat16 [128, 8, 1024], P(('region', 'cluster'))
- residual: float32 [128, 8, 1024], P(('region', 'cluster'))
- posterior: float32 [65536], P(('region', 'cluster'))
Inputs may be any that keep to these rules, and one draw needn't show every extreme that they name: Every draw has some access point with 8 live blocks. `visible`: users are numbered region by region, 2048 * 8 to a region, in the order of the devices along region+cluster. An access point hears only users of its own region or of the two regions beside it along region (the first and the last region are beside each other); most of the users it hears are of its own region.
All inputs are finite; a program needn't handle non-finite values.
Results may differ from a plain program's by a relative error of at most 0.0056.
Values sent between devices are 32-bit elements; how exact they have to be, the bound alone decides.
A program may use at most 192 MiB of HBM per device.

v0:
```python
import jax
import jax.numpy as jnp
from jax import lax
from jax.sharding import PartitionSpec as P

ROW_BLOCK = 128
U_DEV = 2048
epsilon = 1e-06


def passed_along(block, axis, distance):
    devices = range(lax.axis_size(axis))
    route = [((i - distance) % len(devices), i) for i in devices]
    return lax.ppermute(block, axis, route)


def decide(summed, start, count, user_cluster, cluster_prior):
    labels = lax.dynamic_slice_in_dim(user_cluster, start, count)
    table = jnp.arange(cluster_prior.shape[0], dtype=jnp.int32)
    prior = jnp.sum(
        jnp.where(labels[:, None] == table[None, :], cluster_prior[None, :], jnp.float32(0.0)),
        axis=1,
    )
    return jax.nn.sigmoid(summed + prior)


def local(
    pilots, estimate, visible, blocks, received, previous, onsager, user_cluster, cluster_prior
):
    points, antennas, slots = estimate.shape
    live = jnp.arange(slots)[None, :] // ROW_BLOCK < blocks[:, None]
    masked = jnp.where(live[:, None, :], estimate, jnp.zeros_like(estimate))
    widened = masked.astype(jnp.float32)
    product = jnp.einsum("amr,arl->aml", masked, pilots, preferred_element_type=jnp.float32)
    resid = received - product + onsager[:, None, None] * previous
    spread = jnp.mean(resid * resid, axis=(1, 2)) + epsilon
    narrow = resid.astype(jnp.bfloat16)
    stat = widened + jnp.einsum("aml,arl->amr", narrow, pilots, preferred_element_type=jnp.float32)
    energy = jnp.sum(stat * stat, axis=1)
    base = 0.5 * antennas * jnp.log(spread / (1.0 + spread))
    llr = base[:, None] + energy / (2.0 * spread * (1.0 + spread))[:, None]
    llr = jnp.where(live, llr, jnp.float32(0.0))
    total_users = U_DEV * lax.axis_size("region") * lax.axis_size("cluster")
    own_start = lax.axis_index(("region", "cluster")) * U_DEV
    flat_llr = llr.reshape(-1)
    region_users = U_DEV * lax.axis_size("cluster")
    regions = lax.axis_size("region")
    lowest = (lax.axis_index("region") + regions - 1) % regions * region_users
    relative = (visible - lowest + total_users) % total_users
    window = jax.ops.segment_sum(flat_llr, relative.reshape(-1), num_segments=3 * region_users)
    from_below = passed_along(window[2 * region_users :], "region", 1)
    from_above = passed_along(window[:region_users], "region", -1)
    region_sum = window[region_users : 2 * region_users] + from_below + from_above
    owned_sum = lax.psum_scatter(region_sum, "cluster", scatter_dimension=0, tiled=True)
    owned = decide(owned_sum, own_start, U_DEV, user_cluster, cluster_prior)
    own_post = lax.all_gather(owned, "cluster", axis=0, tiled=True)
    below = passed_along(own_post, "region", 1)
    above = passed_along(own_post, "region", -1)
    nearby = jnp.concatenate([below, own_post, above])
    rate = nearby[relative]
    fresh = rate[:, None, :] * stat / (1.0 + spread)[:, None, None]
    new_estimate = jnp.where(live[:, None, :], fresh, jnp.float32(0.0)).astype(jnp.bfloat16)
    return (new_estimate, resid, owned)


def solution(mesh):
    placed = (
        P(("region", "cluster"), None, None),
        P(("region", "cluster"), None, None),
        P(("region", "cluster"), None),
        P(("region", "cluster")),
        P(("region", "cluster"), None, None),
        P(("region", "cluster"), None, None),
        P(("region", "cluster")),
        P(),
        P(),
    )
    return jax.shard_map(
        local,
        mesh=mesh,
        in_specs=placed,
        out_specs=(
            P(("region", "cluster"), None, None),
            P(("region", "cluster"), None, None),
            P(("region", "cluster")),
        ),
        check_vma=False,
    )
```

profile of v0, /device:TPU:0, one launch (start us, length us, event | category | flops | bytes accessed | tf_op | source)
XLA Modules:
  0.0 153.7 jit_solution(528623752502533669)
XLA Ops:
  7.2 0.0 copy-start.2
  7.2 0.0 all-reduce.3.cloned.1.call-start
  7.3 0.0 copy-start
  7.3 0.9 fusion.7
  8.2 0.9 broadcast_compare_fusion
  9.1 0.0 copy-start.4
  9.1 0.0 copy-start.5
  9.1 0.0 copy-start.6
  9.1 5.3 %multiply_reduce_fusion.1 = (f32[4]{0:T(128)S(1)}, f32[4,8,1024]{2,1,0:T(8,128)S(1)}) fusion(f32[4,8,1024]{2,1,0:T(8,128)} %param.14, f32[4]{0:T(128)} %param.15, f32[4,8,1024]{2,1,0:T(8,128)} %param.13, bf16[4,1024,1024]{2,1,0:T(8,128)(2,1)} %param.9, bf16[4,8,1024]{2,1,0:T(8,128)(2,1)} %param.10, pred[4,1024]{1,0:T(4,128)(4,1)S(1)} %broadcast_compare_fusion), kind=kOutput, calls=%fused_computation.10 | convolution fusion | flops 67305472 | bytes 8851488 | tf_op jit(solution)/shard_map/amr,arl->aml/dot_general | solution.py:34
  14.4 0.0 copy-start.1
  14.4 0.0 copy-done.2
  14.4 0.0 copy-done
  14.4 2.3 %multiply_reduce_fusion = (f32[4,1024]{1,0:T(4,128)S(1)}, f32[4,8,1024]{2,1,0:T(8,128)S(1)}) fusion(bf16[4,1024,1024]{2,1,0:T(8,128)(2,1)S(1)} %copy-done, f32[4,8,1024]{2,1,0:T(8,128)S(1)} %get-tuple-element.11, bf16[4,8,1024]{2,1,0:T(8,128)(2,1)S(1)} %copy-done.2, pred[4,1024]{1,0:T(4,128)(4,1)S(1)} %broadcast_compare_fusion), kind=kOutput, calls=%fused_computation.9 | convolution fusion | flops 67301376 | bytes 8736768 | tf_op jit(solution)/shard_map/aml,arl->amr/dot_general | solution.py:38
  16.7 0.0 copy-done.4
  16.7 0.1 select_bitcast_fusion
  16.8 21.9 %scatter_custom_fusion = f32[49152]{0:T(1024)S(1)} fusion(s32[4096]{0:T(1024)S(1)} %bitcast.17, f32[4096]{0:T(1024)S(1)} %bitcast.18, f32[]{:T(128)} %constant.68.clone.1), kind=kCustom, calls=%fused_computation.11 | custom fusion | flops 4096 | bytes 196612 | tf_op jit(solution)/shard_map/scatter-add | solution.py:50
  38.8 3.0 %collective-permute-start = (f32[16384]{0:T(1024)S(1)}, f32[16384]{0:T(1024)S(1)}, u32[]{:S(2)}, u32[]{:S(2)}) collective-permute-start(f32[16384]{0:T(1024)S(1)} %get-tuple-element.3), channel_id=1, source_target_pairs={{24,0},{0,8},{8,16},{16,24},{25,1},{1,9},{9,17},{17,25},{26,2},{2,... | collective-permute-start | bytes 196616 | tf_op jit(solution)/shard_map/ppermute | solution.py:14
  41.8 1.0 collective-permute-start.1
  42.8 0.7 dynamic_slice.3
  43.5 1.6 %collective-permute-done = f32[16384]{0:T(1024)S(1)} collective-permute-done((f32[16384]{0:T(1024)S(1)}, f32[16384]{0:T(1024)S(1)}, u32[]{:S(2)}, u32[]{:S(2)}) %collective-permute-start) | collective-permute-done | bytes 65568 | tf_op jit(solution)/shard_map/ppermute | solution.py:14
  45.1 1.4 collective-permute-done.1
  46.5 0.6 fusion.3
  47.1 0.0 all-reduce.3.cloned.1.call-update
  47.2 0.0 copy-done.5
  47.2 0.1 select_reduce_fusion
  47.3 0.0 copy-done.6
  47.3 0.6 dynamic-slice
  48.5 53.2 %all-reduce.3.cloned.1.call-done = f32[16384]{0:T(1024)} async-done(((f32[16384]{0:T(1024)}), f32[16384]{0:T(1024)}) %all-reduce.3.cloned.1.call-update) | async-done | bytes 65552
  101.7 0.7 fusion.11
  102.4 0.0 copy-start.3
  102.4 14.0 %all_gather.3 = f32[16384]{0:T(1024)S(1)} all-gather(f32[2048]{0:T(1024)S(1)} %fusion.11), channel_id=1, replica_groups=mesh['region'=4,'cluster'=8] {'cluster'}, dimensions={0}, use_global_device_ids=true | all-gather | bytes 73728 | tf_op jit(solution)/shard_map/all_gather | solution.py:56
  116.4 1.5 collective-permute-start.2
  117.8 1.5 collective-permute-start.3
  119.3 2.6 %collective-permute-done.2 = f32[16384]{0:T(1024)S(1)} collective-permute-done((f32[16384]{0:T(1024)S(1)}, f32[16384]{0:T(1024)S(1)}, u32[]{:S(2)}, u32[]{:S(2)}) %collective-permute-start.2) | collective-permute-done | bytes 65568 | tf_op jit(solution)/shard_map/ppermute | solution.py:14
  121.9 1.1 collective-permute-done.3
  123.0 23.0 %gather_fusion = f32[4096]{0:T(1024)S(1)} fusion(f32[49152]{0:T(1024)S(1)} %pad_maximum_fusion, s32[4096]{0:T(1024)S(1)} %bitcast_clamp_fusion), kind=kCustom, calls=%fused_computation | custom fusion | bytes 49152 | tf_op jit(solution)/shard_map/gather | solution.py:60
  146.1 0.0 copy-done.1
  146.1 0.0 copy-done.3
  146.1 0.7 select_convert_fusion
  (8 shorter events, 0.1 us)
Async XLA Ops:
  7.2 7.2 %copy-start.2 = (bf16[4,8,1024]{2,1,0:T(8,128)(2,1)S(1)}, bf16[4,8,1024]{2,1,0:T(8,128)(2,1)}, u32[]{:S(2)}) copy-start(bf16[4,8,1024]{2,1,0:T(8,128)(2,1)} %param.10) | copy-start | bytes 196612
  7.2 94.5 %all-reduce.3.cloned.1.call-start = ((), (), s32[]{:S(2)}) async-start(), calls=%async_computation | async-start | bytes 131072
  7.3 7.1 %copy-start = (bf16[4,1024,1024]{2,1,0:T(8,128)(2,1)S(1)}, bf16[4,1024,1024]{2,1,0:T(8,128)(2,1)}, u32[]{:S(2)}) copy-start(bf16[4,1024,1024]{2,1,0:T(8,128)(2,1)} %param.9) | copy-start | bytes 25165828
  9.1 7.7 %copy-start.4 = (s32[4]{0:T(128)S(1)}, s32[4]{0:T(128)}, u32[]{:S(2)}) copy-start(s32[4]{0:T(128)} %param.12) | copy-start | bytes 52
  9.1 38.1 %copy-start.5 = (f32[16]{0:T(128)S(1)}, f32[16]{0:T(128)}, u32[]{:S(2)}) copy-start(f32[16]{0:T(128)} %param.17) | copy-start | bytes 196
  9.1 38.2 %copy-start.6 = (u32[32]{0:T(128)S(1)}, u32[32]{0:T(128)}, u32[]{:S(2)}) copy-start(u32[32]{0:T(128)} %constant.94) | copy-start | bytes 388
  14.4 131.7 %copy-start.1 = (f32[4,8,1024]{2,1,0:T(8,128)}, f32[4,8,1024]{2,1,0:T(8,128)S(1)}, u32[]{:S(2)}) copy-start(f32[4,8,1024]{2,1,0:T(8,128)S(1)} %get-tuple-element.11) | copy-start | bytes 393220
  38.8 6.3 %collective-permute-start = (f32[16384]{0:T(1024)S(1)}, f32[16384]{0:T(1024)S(1)}, u32[]{:S(2)}, u32[]{:S(2)}) collective-permute-start(f32[16384]{0:T(1024)S(1)} %get-tuple-element.3), channel_id=1, source_target_pairs={{24,0},{0,8},{8,16},{16,24},{25,1},{1,9},{9,17},{17,25},{26,2},{2,... | collective-permute-start | bytes 196616 | tf_op jit(solution)/shard_map/ppermute | solution.py:14
  41.8 4.7 %collective-permute-start.1 = (f32[16384]{0:T(1024)S(1)}, f32[16384]{0:T(1024)S(1)}, u32[]{:S(2)}, u32[]{:S(2)}) collective-permute-start(f32[16384]{0:T(1024)S(1)} %get-tuple-element.4), channel_id=1, source_target_pairs={{8,0},{16,8},{24,16},{0,24},{9,1},{17,9},{25,17},{1,25},{10,2},{18... | collective-permute-start | bytes 196616 | tf_op jit(solution)/shard_map/ppermute | solution.py:14
  102.4 43.7 %copy-start.3 = (f32[2048]{0:T(1024)}, f32[2048]{0:T(1024)S(1)}, u32[]{:S(2)}) copy-start(f32[2048]{0:T(1024)S(1)} %fusion.11) | copy-start | bytes 24580
  116.4 5.5 %collective-permute-start.2 = (f32[16384]{0:T(1024)S(1)}, f32[16384]{0:T(1024)S(1)}, u32[]{:S(2)}, u32[]{:S(2)}) collective-permute-start(f32[16384]{0:T(1024)S(1)} %all_gather.3), channel_id=1, source_target_pairs={{24,0},{0,8},{8,16},{16,24},{25,1},{1,9},{9,17},{17,25},{26,2},{2,... | collective-permute-start | bytes 196616 | tf_op jit(solution)/shard_map/ppermute | solution.py:14
  117.8 5.2 %collective-permute-start.3 = (f32[16384]{0:T(1024)S(1)}, f32[16384]{0:T(1024)S(1)}, u32[]{:S(2)}, u32[]{:S(2)}) collective-permute-start(f32[16384]{0:T(1024)S(1)} %all_gather.3), channel_id=1, source_target_pairs={{8,0},{16,8},{24,16},{0,24},{9,1},{17,9},{25,17},{1,25},{10,2},{18... | collective-permute-start | bytes 196616 | tf_op jit(solution)/shard_map/ppermute | solution.py:14
Sparse Core Ops, SparseCore 0:
  47.3 54.3 all-reduce.2
where the time goes:
time: 154 us
  waiting for transfers between devices  59.9 us (39%)
  other arithmetic  26 us (17%)
  local copies, waits for them, and re-layouts  24.4 us (16%)
  between operations  14.9 us (10%)
  blocking collectives  14 us (9%)
  matrix products  7.59 us (5%)
  starting transfers between devices  6.97 us (5%)
    unnamed x2, waiting for transfers between devices  53.2 us
    gather x2, local copies, waits for them, and re-layouts, local(): rate = nearby[relative]  23 us
    scatter-add x1, other arithmetic, local(): jax.ops.segment_sum(flat_llr, relative.reshape(-1), num_segments=3 * regi...  21.9 us
    all_gather x1, blocking collectives, local(): own_post = lax.all_gather(owned, 'cluster', axis=0, tiled=True)  14 us
    ppermute x4, starting transfers between devices, passed_along(): return lax.ppermute(block, axis, route)  6.94 us
    ppermute x4, waiting for transfers between devices, passed_along(): return lax.ppermute(block, axis, route)  6.68 us
    dot_general x1, matrix products, local(): jnp.einsum('amr,arl->aml', masked, pilots, preferred_element_type=jnp.flo...  5.3 us
  transfers between devices with their start and end apart: 5, of which 5 were waited for; matrix products, arithmetic and copies ran while one was open for 1% of the time, Pallas kernels for 0%

commit v1 on v0

--- a/solution.py
+++ b/solution.py
@@ -6,6 +6,32 @@
 ROW_BLOCK = 128
 U_DEV = 2048
 epsilon = 1e-06
+
+
+def return_all_the_stocks(patch, comm_axis):
+    v_now, r_now, passed = (
+        jax.lax.axis_size(comm_axis),
+        jax.lax.axis_index(comm_axis),
+        patch.shape[0],
+    )
+    fields = [b * v_now if h == 0 else b for h, b in enumerate(patch.shape)]
+    local_part = lax.dynamic_update_slice_in_dim(
+        jnp.zeros(fields, patch.dtype), patch, r_now * passed, axis=0
+    )
+    far_arr = h_now = patch
+    dd = 1
+    while dd < v_now // 2 + 1:
+        far_arr = jax.lax.ppermute(far_arr, comm_axis, [(h, (h + 1) % v_now) for h in range(v_now)])
+        local_part = lax.dynamic_update_slice_in_dim(
+            local_part, far_arr, (r_now - dd) % v_now * passed, axis=0
+        )
+        if 2 * dd < v_now:
+            h_now = jax.lax.ppermute(h_now, comm_axis, [(h, (h - 1) % v_now) for h in range(v_now)])
+            local_part = lax.dynamic_update_slice_in_dim(
+                local_part, h_now, (r_now + dd) % v_now * passed, axis=0
+            )
+        dd += 1
+    return local_part
 
 
 def passed_along(block, axis, distance):
@@ -53,7 +79,7 @@
     region_sum = window[region_users : 2 * region_users] + from_below + from_above
     owned_sum = lax.psum_scatter(region_sum, "cluster", scatter_dimension=0, tiled=True)
     owned = decide(owned_sum, own_start, U_DEV, user_cluster, cluster_prior)
-    own_post = lax.all_gather(owned, "cluster", axis=0, tiled=True)
+    own_post = return_all_the_stocks(owned, "cluster")
     below = passed_along(own_post, "region", 1)
     above = passed_along(own_post, "region", -1)
     nearby = jnp.concatenate([below, own_post, above])

time: 154 us -> 161 us (1.045)
  blocking collectives: 14 us -> 0 us
  starting transfers between devices: 6.97 us -> 17.1 us
  waiting for transfers between devices: 59.9 us -> 68.5 us
  local copies, waits for them, and re-layouts: 24.4 us -> 26.3 us
    all_gather x1 -> x0, blocking collectives: 14 us -> none  [local(): own_post = lax.all_gather(owned, 'cluster', axis=0, tiled=True)]
    ppermute x0 -> x7, starting transfers between devices: none -> 10.6 us  [the longest x3 10.6 us: return_all_the_stocks(): jax.lax.ppermute(h_now, comm_axis, [(h, (h - 1) % v_now) for h in range(v...]
    ppermute x0 -> x7, waiting for transfers between devices: none -> 7.15 us  [the longest x4 7.08 us: return_all_the_stocks(): jax.lax.ppermute(far_arr, comm_axis, [(h, (h + 1) % v_now) for h in range...]
    dynamic_update_slice x0 -> x7, local copies, waits for them, and re-layouts: none -> 1.95 us  [the longest x4 1.03 us: return_all_the_stocks(): lax.dynamic_update_slice_in_dim(local_part, far_arr, (r_now - dd) % v_now...]
  transfers between devices with their start and end apart: 5 -> 12, of which waited for: 5 -> 9; matrix products, arithmetic and copies ran while one was open for 1% -> 2% of each run, Pallas kernels for 0% -> 0%
where the time goes in v1:
time: 161 us; the launch traced here: 160 us
  waiting for transfers between devices  68.5 us (43%)
  local copies, waits for them, and re-layouts  26.3 us (16%)
  other arithmetic  26 us (16%)
  starting transfers between devices  17.1 us (11%)
  between operations  14.9 us (9%)
  matrix products  7.59 us (5%)
    unnamed x2, waiting for transfers between devices  53.2 us
    gather x2, local copies, waits for them, and re-layouts, local(): rate = nearby[relative]  23 us
    scatter-add x1, other arithmetic, local(): jax.ops.segment_sum(flat_llr, relative.reshape(-1), num_segments=3 * regi...  21.9 us
    ppermute x3, starting transfers between devices, return_all_the_stocks(): jax.lax.ppermute(h_now, comm_axis, [(h, (h - 1) % v_now) for h in range(v...  10.6 us
    ppermute x4, waiting for transfers between devices, passed_along(): return lax.ppermute(block, axis, route)  8.14 us
    ppermute x4, waiting for transfers between devices, return_all_the_stocks(): jax.lax.ppermute(far_arr, comm_axis, [(h, (h + 1) % v_now) for h in range...  7.08 us
    ppermute x4, starting transfers between devices, passed_along(): return lax.ppermute(block, axis, route)  6.43 us
    dot_general x1, matrix products, local(): jnp.einsum('amr,arl->aml', masked, pilots, preferred_element_type=jnp.flo...  5.3 us
  transfers between devices with their start and end apart: 12, of which 9 were waited for; matrix products, arithmetic and copies ran while one was open for 2% of the time, Pallas kernels for 0%

profile of v1, /device:TPU:0, one launch (start us, length us, event | category | flops | bytes accessed | tf_op | source)
XLA Modules:
  0.0 160.4 jit_solution(2412965320872709146)
XLA Ops:
  7.2 0.0 copy-start.2
  7.2 0.0 all-reduce.3.cloned.1.call-start
  7.3 0.0 copy-start
  7.3 0.9 fusion.7
  8.2 0.9 broadcast_compare_fusion
  9.1 0.0 copy-start.6
  9.1 5.3 %multiply_reduce_fusion.1 = (f32[4]{0:T(128)S(1)}, f32[4,8,1024]{2,1,0:T(8,128)S(1)}) fusion(f32[4,8,1024]{2,1,0:T(8,128)} %param.14, f32[4]{0:T(128)} %param.15, f32[4,8,1024]{2,1,0:T(8,128)} %param.13, bf16[4,1024,1024]{2,1,0:T(8,128)(2,1)} %param.9, bf16[4,8,1024]{2,1,0:T(8,128)(2,1)} %param.10, pred[4,1024]{1,0:T(4,128)(4,1)S(1)} %broadcast_compare_fusion), kind=kOutput, calls=%fused_computation.10 | convolution fusion | flops 67305472 | bytes 8851488 | tf_op jit(solution)/shard_map/amr,arl->aml/dot_general | solution.py:60
  14.4 2.3 %multiply_reduce_fusion = (f32[4,1024]{1,0:T(4,128)S(1)}, f32[4,8,1024]{2,1,0:T(8,128)S(1)}) fusion(bf16[4,1024,1024]{2,1,0:T(8,128)(2,1)S(1)} %copy-done, f32[4,8,1024]{2,1,0:T(8,128)S(1)} %get-tuple-element.13, bf16[4,8,1024]{2,1,0:T(8,128)(2,1)S(1)} %copy-done.2, pred[4,1024]{1,0:T(4,128)(4,1)S(1)} %broadcast_compare_fusion), kind=kOutput, calls=%fused_computation.9 | convolution fusion | flops 67301376 | bytes 8736768 | tf_op jit(solution)/shard_map/aml,arl->amr/dot_general | solution.py:64
  16.7 0.1 select_bitcast_fusion
  16.8 21.9 %scatter_custom_fusion = f32[49152]{0:T(1024)S(1)} fusion(s32[4096]{0:T(1024)S(1)} %bitcast.17, f32[4096]{0:T(1024)S(1)} %bitcast.18, f32[]{:T(128)} %constant.105.clone.1), kind=kCustom, calls=%fused_computation.11 | custom fusion | flops 4096 | bytes 196612 | tf_op jit(solution)/shard_map/scatter-add | solution.py:76
  38.8 3.0 %collective-permute-start = (f32[16384]{0:T(1024)S(1)}, f32[16384]{0:T(1024)S(1)}, u32[]{:S(2)}, u32[]{:S(2)}) collective-permute-start(f32[16384]{0:T(1024)S(1)} %get-tuple-element.5), channel_id=1, source_target_pairs={{24,0},{0,8},{8,16},{16,24},{25,1},{1,9},{9,17},{17,25},{26,2},{2,... | collective-permute-start | bytes 196616 | tf_op jit(solution)/shard_map/ppermute | solution.py:40
  41.8 1.0 collective-permute-start.1
  42.8 0.7 dynamic_slice.3
  43.5 1.6 %collective-permute-done = f32[16384]{0:T(1024)S(1)} collective-permute-done((f32[16384]{0:T(1024)S(1)}, f32[16384]{0:T(1024)S(1)}, u32[]{:S(2)}, u32[]{:S(2)}) %collective-permute-start) | collective-permute-done | bytes 65568 | tf_op jit(solution)/shard_map/ppermute | solution.py:40
  45.1 1.4 collective-permute-done.1
  46.5 0.6 fusion.3
  47.1 0.0 all-reduce.3.cloned.1.call-update
  47.2 0.1 select_reduce_fusion
  47.3 0.6 dynamic-slice
  48.5 53.2 %all-reduce.3.cloned.1.call-done = f32[16384]{0:T(1024)} async-done(((f32[16384]{0:T(1024)}), f32[16384]{0:T(1024)}) %all-reduce.3.cloned.1.call-update) | async-done | bytes 65552
  101.7 0.7 fusion.17
  102.4 0.1 collective-permute-start.2
  102.5 3.5 %collective-permute-start.3 = (f32[2048]{0:T(1024)S(1)}, f32[2048]{0:T(1024)S(1)}, u32[]{:S(2)}, u32[]{:S(2)}) collective-permute-start(f32[2048]{0:T(1024)S(1)} %get-tuple-element.4), channel_id=1, source_target_pairs={{0,7},{1,0},{2,1},{3,2},{4,3},{5,4},{6,5},{7,6},{8,15},{9,8},{10,9... | collective-permute-start | bytes 24584 | tf_op jit(solution)/shard_map/ppermute | solution.py:29
  106.0 1.3 collective-permute-done.2
  107.3 0.0 collective-permute-start.4
  107.3 0.0 collective-permute-done.3
  107.4 3.5 %collective-permute-start.5 = (f32[2048]{0:T(1024)S(1)}, f32[2048]{0:T(1024)S(1)}, u32[]{:S(2)}, u32[]{:S(2)}) collective-permute-start(f32[2048]{0:T(1024)S(1)} %collective-permute-done.3), channel_id=1, source_target_pairs={{0,7},{1,0},{2,1},{3,2},{4,3},{5,4},{6,5},{7,6},{8,15},{9,8},{10,9... | collective-permute-start | bytes 24584 | tf_op jit(solution)/shard_map/ppermute | solution.py:29
  110.9 1.3 collective-permute-done.4
  112.2 0.0 collective-permute-start.6
  112.2 0.0 collective-permute-done.5
  112.2 3.5 %collective-permute-start.7 = (f32[2048]{0:T(1024)S(1)}, f32[2048]{0:T(1024)S(1)}, u32[]{:S(2)}, u32[]{:S(2)}) collective-permute-start(f32[2048]{0:T(1024)S(1)} %collective-permute-done.5), channel_id=1, source_target_pairs={{0,7},{1,0},{2,1},{3,2},{4,3},{5,4},{6,5},{7,6},{8,15},{9,8},{10,9... | collective-permute-start | bytes 24584 | tf_op jit(solution)/shard_map/ppermute | solution.py:29
  115.8 1.3 collective-permute-done.6
  117.1 0.0 collective-permute-start.8
  117.1 0.2 dynamic_update_slice.25
  117.3 0.3 dynamic_update_slice.26
  117.6 0.3 dynamic_update_slice.27
  117.9 0.3 dynamic_update_slice.28
  118.2 0.3 dynamic_update_slice.29
  118.5 0.0 collective-permute-done.7
  118.5 0.3 dynamic_update_slice.30
  118.9 3.1 %collective-permute-done.8 = f32[2048]{0:T(1024)S(1)} collective-permute-done((f32[2048]{0:T(1024)S(1)}, f32[2048]{0:T(1024)S(1)}, u32[]{:S(2)}, u32[]{:S(2)}) %collective-permute-start.8) | collective-permute-done | bytes 8224 | tf_op jit(solution)/shard_map/ppermute | solution.py:24
  122.0 0.2 dynamic_update_slice.31
  122.1 2.4 %collective-permute-start.10 = (f32[16384]{0:T(1024)S(1)}, f32[16384]{0:T(1024)S(1)}, u32[]{:S(2)}, u32[]{:S(2)}) collective-permute-start(f32[16384]{0:T(1024)S(1)} %dynamic_update_slice.31), channel_id=1, source_target_pairs={{8,0},{16,8},{24,16},{0,24},{9,1},{17,9},{25,17},{1,25},{10,2},{18... | collective-permute-start | bytes 196616 | tf_op jit(solution)/shard_map/ppermute | solution.py:40
  124.6 0.0 collective-permute-start.9
  124.6 1.9 %collective-permute-done.10 = f32[16384]{0:T(1024)S(1)} collective-permute-done((f32[16384]{0:T(1024)S(1)}, f32[16384]{0:T(1024)S(1)}, u32[]{:S(2)}, u32[]{:S(2)}) %collective-permute-start.10) | collective-permute-done | bytes 65568 | tf_op jit(solution)/shard_map/ppermute | solution.py:40
  126.5 3.3 %collective-permute-done.9 = f32[16384]{0:T(1024)S(1)} collective-permute-done((f32[16384]{0:T(1024)S(1)}, f32[16384]{0:T(1024)S(1)}, u32[]{:S(2)}, u32[]{:S(2)}) %collective-permute-start.9) | collective-permute-done | bytes 65568 | tf_op jit(solution)/shard_map/ppermute | solution.py:40
  129.7 23.0 %gather_fusion = f32[4096]{0:T(1024)S(1)} fusion(f32[49152]{0:T(1024)S(1)} %pad_maximum_fusion, s32[4096]{0:T(1024)S(1)} %bitcast_clamp_fusion), kind=kCustom, calls=%fused_computation | custom fusion | bytes 49152 | tf_op jit(solution)/shard_map/gather | solution.py:86
  152.8 0.7 select_convert_fusion
  (20 shorter events, 0.1 us)
Async XLA Ops:
  7.2 7.2 %copy-start.2 = (bf16[4,8,1024]{2,1,0:T(8,128)(2,1)S(1)}, bf16[4,8,1024]{2,1,0:T(8,128)(2,1)}, u32[]{:S(2)}) copy-start(bf16[4,8,1024]{2,1,0:T(8,128)(2,1)} %param.10) | copy-start | bytes 196612
  7.2 94.5 %all-reduce.3.cloned.1.call-start = ((), (), s32[]{:S(2)}) async-start(), calls=%async_computation | async-start | bytes 131072
  7.3 7.1 %copy-start = (bf16[4,1024,1024]{2,1,0:T(8,128)(2,1)S(1)}, bf16[4,1024,1024]{2,1,0:T(8,128)(2,1)}, u32[]{:S(2)}) copy-start(bf16[4,1024,1024]{2,1,0:T(8,128)(2,1)} %param.9) | copy-start | bytes 25165828
  9.1 7.7 %copy-start.4 = (s32[4]{0:T(128)S(1)}, s32[4]{0:T(128)}, u32[]{:S(2)}) copy-start(s32[4]{0:T(128)} %param.12) | copy-start | bytes 52
  9.1 38.1 %copy-start.5 = (f32[16]{0:T(128)S(1)}, f32[16]{0:T(128)}, u32[]{:S(2)}) copy-start(f32[16]{0:T(128)} %param.17) | copy-start | bytes 196
  9.1 38.2 %copy-start.6 = (u32[32]{0:T(128)S(1)}, u32[32]{0:T(128)}, u32[]{:S(2)}) copy-start(u32[32]{0:T(128)} %constant.136) | copy-start | bytes 388
  14.4 138.4 %copy-start.1 = (f32[4,8,1024]{2,1,0:T(8,128)}, f32[4,8,1024]{2,1,0:T(8,128)S(1)}, u32[]{:S(2)}) copy-start(f32[4,8,1024]{2,1,0:T(8,128)S(1)} %get-tuple-element.13) | copy-start | bytes 393220
  38.8 6.3 %collective-permute-start = (f32[16384]{0:T(1024)S(1)}, f32[16384]{0:T(1024)S(1)}, u32[]{:S(2)}, u32[]{:S(2)}) collective-permute-start(f32[16384]{0:T(1024)S(1)} %get-tuple-element.5), channel_id=1, source_target_pairs={{24,0},{0,8},{8,16},{16,24},{25,1},{1,9},{9,17},{17,25},{26,2},{2,... | collective-permute-start | bytes 196616 | tf_op jit(solution)/shard_map/ppermute | solution.py:40
  41.8 4.7 %collective-permute-start.1 = (f32[16384]{0:T(1024)S(1)}, f32[16384]{0:T(1024)S(1)}, u32[]{:S(2)}, u32[]{:S(2)}) collective-permute-start(f32[16384]{0:T(1024)S(1)} %get-tuple-element.6), channel_id=1, source_target_pairs={{8,0},{16,8},{24,16},{0,24},{9,1},{17,9},{25,17},{1,25},{10,2},{18... | collective-permute-start | bytes 196616 | tf_op jit(solution)/shard_map/ppermute | solution.py:40
  102.4 50.4 %copy-start.3 = (f32[2048]{0:T(1024)}, f32[2048]{0:T(1024)S(1)}, u32[]{:S(2)}) copy-start(f32[2048]{0:T(1024)S(1)} %get-tuple-element.4) | copy-start | bytes 24580
  102.4 4.9 %collective-permute-start.2 = (f32[2048]{0:T(1024)S(1)}, f32[2048]{0:T(1024)S(1)}, u32[]{:S(2)}, u32[]{:S(2)}) collective-permute-start(f32[2048]{0:T(1024)S(1)} %get-tuple-element.4), channel_id=1, source_target_pairs={{0,1},{1,2},{2,3},{3,4},{4,5},{5,6},{6,7},{7,0},{8,9},{9,10},{10,1... | collective-permute-start | bytes 24584 | tf_op jit(solution)/shard_map/ppermute | solution.py:24
  102.5 4.9 %collective-permute-start.3 = (f32[2048]{0:T(1024)S(1)}, f32[2048]{0:T(1024)S(1)}, u32[]{:S(2)}, u32[]{:S(2)}) collective-permute-start(f32[2048]{0:T(1024)S(1)} %get-tuple-element.4), channel_id=1, source_target_pairs={{0,7},{1,0},{2,1},{3,2},{4,3},{5,4},{6,5},{7,6},{8,15},{9,8},{10,9... | collective-permute-start | bytes 24584 | tf_op jit(solution)/shard_map/ppermute | solution.py:29
  107.3 4.9 %collective-permute-start.4 = (f32[2048]{0:T(1024)S(1)}, f32[2048]{0:T(1024)S(1)}, u32[]{:S(2)}, u32[]{:S(2)}) collective-permute-start(f32[2048]{0:T(1024)S(1)} %collective-permute-done.2), channel_id=1, source_target_pairs={{0,1},{1,2},{2,3},{3,4},{4,5},{5,6},{6,7},{7,0},{8,9},{9,10},{10,1... | collective-permute-start | bytes 24584 | tf_op jit(solution)/shard_map/ppermute | solution.py:24
  107.4 4.9 %collective-permute-start.5 = (f32[2048]{0:T(1024)S(1)}, f32[2048]{0:T(1024)S(1)}, u32[]{:S(2)}, u32[]{:S(2)}) collective-permute-start(f32[2048]{0:T(1024)S(1)} %collective-permute-done.3), channel_id=1, source_target_pairs={{0,7},{1,0},{2,1},{3,2},{4,3},{5,4},{6,5},{7,6},{8,15},{9,8},{10,9... | collective-permute-start | bytes 24584 | tf_op jit(solution)/shard_map/ppermute | solution.py:29
  112.2 4.9 %collective-permute-start.6 = (f32[2048]{0:T(1024)S(1)}, f32[2048]{0:T(1024)S(1)}, u32[]{:S(2)}, u32[]{:S(2)}) collective-permute-start(f32[2048]{0:T(1024)S(1)} %collective-permute-done.4), channel_id=1, source_target_pairs={{0,1},{1,2},{2,3},{3,4},{4,5},{5,6},{6,7},{7,0},{8,9},{9,10},{10,1... | collective-permute-start | bytes 24584 | tf_op jit(solution)/shard_map/ppermute | solution.py:24
  112.2 6.3 %collective-permute-start.7 = (f32[2048]{0:T(1024)S(1)}, f32[2048]{0:T(1024)S(1)}, u32[]{:S(2)}, u32[]{:S(2)}) collective-permute-start(f32[2048]{0:T(1024)S(1)} %collective-permute-done.5), channel_id=1, source_target_pairs={{0,7},{1,0},{2,1},{3,2},{4,3},{5,4},{6,5},{7,6},{8,15},{9,8},{10,9... | collective-permute-start | bytes 24584 | tf_op jit(solution)/shard_map/ppermute | solution.py:29
  117.1 4.9 %collective-permute-start.8 = (f32[2048]{0:T(1024)S(1)}, f32[2048]{0:T(1024)S(1)}, u32[]{:S(2)}, u32[]{:S(2)}) collective-permute-start(f32[2048]{0:T(1024)S(1)} %collective-permute-done.6), channel_id=1, source_target_pairs={{0,1},{1,2},{2,3},{3,4},{4,5},{5,6},{6,7},{7,0},{8,9},{9,10},{10,1... | collective-permute-start | bytes 24584 | tf_op jit(solution)/shard_map/ppermute | solution.py:24
  122.1 4.3 %collective-permute-start.10 = (f32[16384]{0:T(1024)S(1)}, f32[16384]{0:T(1024)S(1)}, u32[]{:S(2)}, u32[]{:S(2)}) collective-permute-start(f32[16384]{0:T(1024)S(1)} %dynamic_update_slice.31), channel_id=1, source_target_pairs={{8,0},{16,8},{24,16},{0,24},{9,1},{17,9},{25,17},{1,25},{10,2},{18... | collective-permute-start | bytes 196616 | tf_op jit(solution)/shard_map/ppermute | solution.py:40
  124.6 5.2 %collective-permute-start.9 = (f32[16384]{0:T(1024)S(1)}, f32[16384]{0:T(1024)S(1)}, u32[]{:S(2)}, u32[]{:S(2)}) collective-permute-start(f32[16384]{0:T(1024)S(1)} %dynamic_update_slice.31), channel_id=1, source_target_pairs={{24,0},{0,8},{8,16},{16,24},{25,1},{1,9},{9,17},{17,25},{26,2},{2,... | collective-permute-start | bytes 196616 | tf_op jit(solution)/shard_map/ppermute | solution.py:40
Sparse Core Ops, SparseCore 0:
  47.3 54.3 all-reduce.2
